TPU v7x, 256 devices: a whole 4x4x8 slice. The times are simulated.
256 devices in a mesh: row: 16 (over x, z_lo), col: 16 (over y, z_hi, core).
Axes of the slice: x: 4, y: 4, z: 8 (z_hi: 2, z_lo: 4; z = z_hi * 4 + z_lo), core: 2. Of those that a mesh axis runs over, the one named last changes fastest.
Arguments:
- potential: float32 [32, 64, 512], P('row', 'col'), may hold values from -6 to 6
- basis: bfloat16 [32, 64, 384, 512], P('row', 'col'), may hold values from -6 to 6
- hamiltonian: bfloat16 [6144, 6144], P('row', 'col'), may hold values from -0.078125 to 0.078125
- density: bfloat16 [2, 6144, 6144], P(None, 'row', 'col'), may hold values from -6 to 6
- hmask: int32 [48, 48], replicated, may hold values from 0 to 1, as said below
- pmask: int32 [48, 48], replicated, may hold values from 0 to 1, as said below
Outputs:
- propagated: bfloat16 [2, 6144, 6144], P(None, 'row', 'col')
Inputs may be any that keep to these rules, and one draw needn't show every extreme that they name: hmask[I, I] is always 1; every other block is 1 with probability 1/2, independently. pmask follows the same law as hmask, drawn independently.
All inputs are finite; a program needn't handle non-finite values.
Results may differ from a plain program's by a relative error of at most 0.0062.
Values may be sent and summed in bfloat16 or wider, within the bound.
A program may use at most 64 MiB of HBM per device.

v0:
```python
import jax
import jax.numpy as jnp
from jax import lax
from jax.sharding import PartitionSpec as P

BLK = 128
KAPPA = 0.4
TIME_STEP = 0.5


def extended_2(block, sides, width):
    for axis, dim in sides:
        count = lax.axis_size(axis)
        forward = [(i, i + 1) for i in range(count - 1)]
        backward = [(target, source) for source, target in forward]
        low = lax.ppermute(
            lax.slice_in_dim(block, block.shape[dim] - width, None, axis=dim), axis, forward
        )
        high = lax.ppermute(lax.slice_in_dim(block, 0, width, axis=dim), axis, backward)
        block = jnp.concatenate([low, block, high], axis=dim)
    return block


def shards(potential, basis, hamiltonian, density, hmask, pmask):
    width_x, width_y, depth_z = potential.shape
    extended = extended_2(potential, (("row", 0), ("col", 1)), 1)
    padded = jnp.pad(extended, ((0, 0), (0, 0), (1, 1)))
    beside = padded[2:, 1:-1, 1:-1] + padded[:-2, 1:-1, 1:-1]
    beside = beside + padded[1:-1, 2:, 1:-1] + padded[1:-1, :-2, 1:-1]
    beside = beside + padded[1:-1, 1:-1, 2:] + padded[1:-1, 1:-1, :-2]
    effective = potential + KAPPA * (beside - 6.0 * potential)
    blocks_here = basis.shape[2] // BLK
    weighted = (basis * effective[:, :, None, :]).astype(jnp.bfloat16)
    partial_blocks = jnp.einsum(
        "xykaz,xykbz->kab",
        weighted.reshape(width_x, width_y, blocks_here, BLK, depth_z),
        basis.reshape(width_x, width_y, blocks_here, BLK, depth_z),
        preferred_element_type=jnp.float32,
    )
    summed = lax.psum(partial_blocks, "col")
    factor = float(BLK * width_x * width_y * depth_z * lax.axis_size("col")) ** (-0.5)
    potential_blocks = (summed * factor).astype(jnp.bfloat16)
    block_total = hmask.shape[0]
    blocks_wide = block_total // lax.axis_size("col")
    row_start = lax.axis_index("row") * blocks_here
    col_start = lax.axis_index("col") * blocks_wide
    hpattern = lax.dynamic_slice(hmask, (row_start, col_start), (blocks_here, blocks_wide))
    ppattern = lax.dynamic_slice(pmask, (row_start, col_start), (blocks_here, blocks_wide))
    masked_h = (
        hamiltonian.reshape(blocks_here, BLK, blocks_wide, BLK)
        * hpattern[:, None, :, None].astype(jnp.bfloat16)
    ).reshape(blocks_here * BLK, blocks_wide * BLK)
    masked_p = (
        density.reshape(2, blocks_here, BLK, blocks_wide, BLK)
        * ppattern[None, :, None, :, None].astype(jnp.bfloat16)
    ).reshape(2, blocks_here * BLK, blocks_wide * BLK)

    def diagonal_term(operand):
        local = jnp.einsum(
            "kab,skbc->skac",
            potential_blocks,
            operand.reshape(2, blocks_here, BLK, operand.shape[2]),
            preferred_element_type=jnp.float32,
        )
        return local.reshape(2, blocks_here * BLK, operand.shape[2])

    def apply(operand):
        column_whole = lax.all_gather(operand, "row", axis=1, tiled=True)
        remote = jnp.einsum(
            "rk,skc->src",
            lax.all_gather(masked_h, "col", axis=1, tiled=True),
            column_whole,
            preferred_element_type=jnp.float32,
        )
        return remote + diagonal_term(operand)

    first = apply(masked_p)
    first_rounded = first.astype(jnp.bfloat16)
    second = apply(first_rounded)
    base = masked_p.astype(jnp.float32)
    half_square = 0.5 * TIME_STEP * TIME_STEP
    real_part = base[0] + TIME_STEP * first[1] - half_square * second[0]
    imag_part = base[1] - TIME_STEP * first[0] - half_square * second[1]
    stacked = jnp.stack([real_part, imag_part]).reshape(2, blocks_here, BLK, blocks_wide, BLK)
    stacked = stacked * ppattern[None, :, None, :, None].astype(jnp.float32)
    return stacked.reshape(2, blocks_here * BLK, blocks_wide * BLK).astype(jnp.bfloat16)


def solution(mesh):
    in_specs = (
        P("row", "col", None),
        P("row", "col", None, None),
        P("row", "col"),
        P(None, "row", "col"),
        P(),
        P(),
    )
    out_specs = P(None, "row", "col")
    return jax.shard_map(shards, mesh=mesh, in_specs=in_specs, out_specs=out_specs, check_vma=False)
```

profile of v0, /device:TPU:1, one launch (start us, length us, event | category | flops | bytes accessed | tf_op | source)
XLA Modules:
  0.0 729.8 jit_solution(5748484860902074060)
XLA Ops:
  6.5 0.7 fusion.37
  7.3 4.3 collective-permute-start.1
  11.6 1.3 collective-permute-start
  12.9 0.7 constant_dynamic-update-slice_fusion.1
  13.7 2.5 collective-permute-done
  16.2 3.8 collective-permute-start.2
  20.1 7.8 %collective-permute-start.3 = (f32[4,1,512]{2,1,0:T(1,128)S(1)}, f32[4,1,512]{2,1,0:T(1,128)S(1)}, u32[]{:S(2)}, u32[]{:S(2)}) collective-permute-start(f32[4,1,512]{2,1,0:T(1,128)S(1)} %get-tuple-element.9), channel_id=1, source_target_pairs={{0,1},{1,2},{2,3},{3,4},{4,5},{5,6},{6,7},{7,8},{8,9},{9,10},{10,1... | collective-permute-start | bytes 24584 | tf_op jit(solution)/shard_map/ppermute | solution.py:16
  27.9 0.8 dynamic-slice_convert_fusion.1
  28.8 0.9 fusion.29
  29.7 2.7 multiply_convert_fusion
  32.6 1.7 convolution_bitcast_fusion.2
  34.5 0.8 bitcast_multiply_fusion
  35.6 0.9 fusion.35
  36.7 175.1 %all-reduce.3.cloned.1.call-done = f32[3,128,128]{2,1,0:T(8,128)} async-done(((f32[3,128,128]{2,1,0:T(8,128)}), f32[3,128,128]{2,1,0:T(8,128)}) %all-reduce.3.cloned.1.call-update) | async-done | bytes 196624 | tf_op jit(solution)/shard_map/psum | solution.py:40
  211.8 1.2 convolution_bitcast_fusion.1
  213.2 82.5 %all-gather.6.cloned.1.call-done = bf16[384,6144]{1,0:T(8,128)(2,1)} async-done(((bf16[384,384]{1,0:T(8,128)(2,1)}), bf16[384,6144]{1,0:T(8,128)(2,1)}) %all-gather.6.cloned.1.call-update) | async-done | bytes 4718608 | tf_op jit(solution)/shard_map/all_gather | solution.py:71
  295.7 203.1 %all-gather.4.cloned.1.call-done = bf16[2,6144,384]{2,1,0:T(8,128)(2,1)} async-done(((bf16[2,384,384]{2,1,0:T(8,128)(2,1)}), bf16[2,6144,384]{2,1,0:T(8,128)(2,1)}) %all-gather.4.cloned.1.call-update) | async-done | bytes 9437200 | tf_op jit(solution)/shard_map/all_gather | solution.py:68
  498.8 10.2 %fusion.38 = (bf16[2,384,384]{2,1,0:T(8,128)(2,1)}, f32[2,384,384]{2,1,0:T(8,128)}) fusion(f32[2,384,384]{2,1,0:T(8,128)S(1)} %bitcast.74, bf16[2,6144,384]{2,1,0:T(8,128)(2,1)} %all-gather.4.cloned.1.call-done, bf16[384,6144]{1,0:T(8,128)(2,1)} %all-gather.6.cloned.1.call-done), kind=kOutput, calls=%fused_computation.61 | convolution fusion | flops 3624468480 | bytes 17104896 | tf_op jit(solution)/shard_map/rk,skc->src/dot_general | solution.py:69
  509.2 0.8 copy-done.1
  510.0 0.3 convolution_bitcast_fusion
  510.4 203.2 %all-gather.8.cloned.1.call-done = bf16[2,6144,384]{2,1,0:T(8,128)(2,1)} async-done(((bf16[2,384,384]{2,1,0:T(8,128)(2,1)}), bf16[2,6144,384]{2,1,0:T(8,128)(2,1)}) %all-gather.8.cloned.1.call-update) | async-done | bytes 9437200 | tf_op jit(solution)/shard_map/all_gather | solution.py:68
  713.6 8.5 %fusion.13 = f32[2,384,384]{2,1,0:T(8,128)S(1)} fusion(f32[2,384,384]{2,1,0:T(8,128)S(1)} %bitcast.75, bf16[2,6144,384]{2,1,0:T(8,128)(2,1)} %all-gather.8.cloned.1.call-done, bf16[384,6144]{1,0:T(8,128)(2,1)} %all-gather.6.cloned.1.call-done), kind=kOutput, calls=%fused_computation.10 | convolution fusion | flops 3624173568 | bytes 16515072 | tf_op jit(solution)/shard_map/rk,skc->src/dot_general | solution.py:69
  722.1 0.3 fusion.19
  722.4 0.9 fusion.16
  (35 shorter events, 1.3 us)
Async XLA Ops:
  6.5 205.3 %all-reduce.3.cloned.1.call-start = ((), (), s32[]{:S(2)}) async-start(), calls=%async_computation.2 | async-start | bytes 393216 | tf_op jit(solution)/shard_map/psum | solution.py:40
  7.3 5.7 collective-permute-start.1
  11.6 4.6 collective-permute-start
  16.2 12.5 %collective-permute-start.2 = (f32[4,1,512]{2,1,0:T(1,128)S(1)}, f32[4,1,512]{2,1,0:T(1,128)S(1)}, u32[]{:S(2)}, u32[]{:S(2)}) collective-permute-start(f32[4,1,512]{2,1,0:T(1,128)S(1)} %get-tuple-element.10), channel_id=1, source_target_pairs={{1,0},{2,1},{3,2},{4,3},{5,4},{6,5},{7,6},{8,7},{9,8},{10,9},{11,1... | collective-permute-start | bytes 24584 | tf_op jit(solution)/shard_map/ppermute | solution.py:19
  20.1 8.6 %collective-permute-start.3 = (f32[4,1,512]{2,1,0:T(1,128)S(1)}, f32[4,1,512]{2,1,0:T(1,128)S(1)}, u32[]{:S(2)}, u32[]{:S(2)}) collective-permute-start(f32[4,1,512]{2,1,0:T(1,128)S(1)} %get-tuple-element.9), channel_id=1, source_target_pairs={{0,1},{1,2},{2,3},{3,4},{4,5},{5,6},{6,7},{7,8},{8,9},{9,10},{10,1... | collective-permute-start | bytes 24584 | tf_op jit(solution)/shard_map/ppermute | solution.py:16
  29.7 2.8 copy-start
  32.6 1.9 copy-start.5
  32.6 3.0 copy-start.2
  34.2 261.5 %all-gather.6.cloned.1.call-start = ((), (), s32[]{:S(2)}) async-start(), calls=%async_computation.1 | async-start | bytes 5013504 | tf_op jit(solution)/shard_map/all_gather | solution.py:71
  35.3 463.5 %all-gather.4.cloned.1.call-start = ((), (), s32[]{:S(2)}) async-start(), calls=%async_computation | async-start | bytes 10027008 | tf_op jit(solution)/shard_map/all_gather | solution.py:68
  36.6 677.0 %all-gather.8.cloned.1.call-start = ((), (), s32[]{:S(2)}) async-start(), calls=%async_computation.3 | async-start | bytes 10027008 | tf_op jit(solution)/shard_map/all_gather | solution.py:68
  498.8 10.4 %copy-start.4 = (f32[3,128,128]{2,1,0:T(8,128)S(1)}, f32[3,128,128]{2,1,0:T(8,128)}, u32[]{:S(2)}) copy-start(f32[3,128,128]{2,1,0:T(8,128)} %all-reduce.3.cloned.1.call-done) | copy-start | bytes 589828
  508.9 1.1 copy-start.1
  713.6 8.5 %copy-start.3 = (f32[2,384,384]{2,1,0:T(8,128)S(1)}, f32[2,384,384]{2,1,0:T(8,128)}, u32[]{:S(2)}) copy-start(f32[2,384,384]{2,1,0:T(8,128)} %get-tuple-element.16) | copy-start | bytes 3538948
Sparse Core Ops, SparseCore 0:
  34.4 177.4 all-reduce.2
  214.4 81.2 all-gather.5
  297.5 201.2 all-gather.3
  509.1 204.4 all-gather.7
where the time goes:
time: 730 us
  waiting for transfers between devices  667 us (91%)
  matrix products  21.9 us (3%)
  starting transfers between devices  17.4 us (2%)
  between operations  13.3 us (2%)
  other arithmetic  7.46 us (1%)
    all_gather x2, waiting for transfers between devices, apply(): column_whole = lax.all_gather(operand, 'row', axis=1, tiled=True)  406 us
    psum x1, waiting for transfers between devices, shards(): summed = lax.psum(partial_blocks, 'col')  175 us
    all_gather x1, waiting for transfers between devices, apply(): lax.all_gather(masked_h, 'col', axis=1, tiled=True)  82.5 us
    dot_general x2, matrix products, apply(): jnp.einsum('rk,skc->src', lax.all_gather(masked_h, 'col', axis=1, tiled=T...  18.7 us
  transfers between devices with their start and end apart: 8, of which 5 were waited for; matrix products, arithmetic and copies ran while one was open for 1% of the time, Pallas kernels for 0%

commit v1 on v0

--- a/solution.py
+++ b/solution.py
@@ -68,7 +68,9 @@
         column_whole = lax.all_gather(operand, "row", axis=1, tiled=True)
         remote = jnp.einsum(
             "rk,skc->src",
-            lax.all_gather(masked_h, "col", axis=1, tiled=True),
+            jnp.concatenate(
+                lax.all_to_all(jnp.stack([masked_h] * lax.axis_size("col")), "col", 0, 0), axis=1
+            ),
             column_whole,
             preferred_element_type=jnp.float32,
         )

time: 730 us -> 689 us (0.944)
  waiting for transfers between devices: 667 us -> 596 us
  local copies, waits for them, and re-layouts: 3.23 us -> 20.9 us
  starting transfers between devices: 17.4 us -> 27.8 us
    psum x1, waiting for transfers between devices: 175 us -> 389 us  [shards(): summed = lax.psum(partial_blocks, 'col')]
    all_gather x2, waiting for transfers between devices: 406 us -> 204 us  [apply(): column_whole = lax.all_gather(operand, 'row', axis=1, tiled=True)]
    all_gather x1 -> x0, waiting for transfers between devices: 82.5 us -> none  [apply(): lax.all_gather(masked_h, 'col', axis=1, tiled=True)]
    reshape x0 -> x2, local copies, waits for them, and re-layouts: none -> 15 us  [apply(): jnp.concatenate(lax.all_to_all(jnp.stack([masked_h] * lax.axis_size('col'...]
    all_to_all x0 -> x1, starting transfers between devices: none -> 10.2 us  [apply(): lax.all_to_all(jnp.stack([masked_h] * lax.axis_size('col')), 'col', 0, 0)]
  transfers between devices with their start and end apart: 8 -> 8, of which waited for: 5 -> 3; matrix products, arithmetic and copies ran while one was open for 1% -> 3% of each run, Pallas kernels for 0% -> 0%
where the time goes in v1:
time: 689 us; the launch traced here: 688 us
  waiting for transfers between devices  596 us (87%)
  starting transfers between devices  27.8 us (4%)
  matrix products  21.9 us (3%)
  local copies, waits for them, and re-layouts  20.9 us (3%)
  between operations  15.1 us (2%)
    psum x1, waiting for transfers between devices, shards(): summed = lax.psum(partial_blocks, 'col')  389 us
    all_gather x2, waiting for transfers between devices, apply(): column_whole = lax.all_gather(operand, 'row', axis=1, tiled=True)  204 us
    dot_general x2, matrix products, apply(): jnp.einsum('rk,skc->src', jnp.concatenate(lax.all_to_all(jnp.stack([maske...  18.7 us
    reshape x2, local copies, waits for them, and re-layouts, apply(): jnp.concatenate(lax.all_to_all(jnp.stack([masked_h] * lax.axis_size('col'...  15 us
  transfers between devices with their start and end apart: 8, of which 3 were waited for; matrix products, arithmetic and copies ran while one was open for 3% of the time, Pallas kernels for 0%

profile of v1, /device:TPU:1, one launch (start us, length us, event | category | flops | bytes accessed | tf_op | source)
XLA Modules:
  0.0 688.0 jit_solution(5584592579149452182)
XLA Ops:
  7.4 0.7 fusion.23
  8.1 4.3 collective-permute-start.1
  12.4 1.3 collective-permute-start
  13.8 0.7 constant_dynamic-update-slice_fusion.1
  14.5 2.5 collective-permute-done
  17.1 3.8 collective-permute-start.2
  20.9 7.8 %collective-permute-start.3 = (f32[4,1,512]{2,1,0:T(1,128)S(1)}, f32[4,1,512]{2,1,0:T(1,128)S(1)}, u32[]{:S(2)}, u32[]{:S(2)}) collective-permute-start(f32[4,1,512]{2,1,0:T(1,128)S(1)} %get-tuple-element.9), channel_id=1, source_target_pairs={{0,1},{1,2},{2,3},{3,4},{4,5},{5,6},{6,7},{7,8},{8,9},{9,10},{10,1... | collective-permute-start | bytes 24584 | tf_op jit(solution)/shard_map/ppermute | solution.py:16
  28.7 0.8 dynamic-slice_convert_fusion.1
  29.9 0.9 fusion.15
  30.8 2.7 multiply_convert_fusion
  33.6 1.7 convolution_bitcast_fusion.4
  35.4 0.9 fusion.21
  36.6 2.7 stack.4
  39.3 10.2 %all-to-all-start = ((bf16[16,384,384]{2,1,0:T(8,128)(2,1)}), bf16[16,384,384]{2,1,0:T(8,128)(2,1)}, u32[]{:S(2)}, u32[]{:S(2)}) async-start(bf16[16,384,384]{2,1,0:T(8,128)(2,1)} %stack.4), calls=%async_computation | async-start | bytes 9437184 | tf_op jit(solution)/shard_map/all_to_all | solution.py:72
  49.9 389.2 %all-reduce.3.cloned.1.call-done = f32[3,128,128]{2,1,0:T(8,128)} async-done(((f32[3,128,128]{2,1,0:T(8,128)}), f32[3,128,128]{2,1,0:T(8,128)}) %all-reduce.3.cloned.1.call-update) | async-done | bytes 196624 | tf_op jit(solution)/shard_map/psum | solution.py:40
  439.1 1.2 convolution_bitcast_fusion.2
  440.4 7.2 %copy.23 = bf16[384,16,384]{2,1,0:T(8,128)(2,1)} copy(bf16[384,16,384]{2,0,1:T(8,128)(2,1)} %bitcast) | data formatting | bytes 9437184 | tf_op jit(solution)/shard_map/reshape | solution.py:71
  447.7 7.7 %reshape.59 = bf16[384,6144,1]{1,0,2:T(8,128)(2,1)} reshape(bf16[384,16,384]{2,1,0:T(8,128)(2,1)} %copy.23) | data formatting | bytes 9437184 | tf_op jit(solution)/shard_map/reshape | solution.py:71
  455.4 10.2 %fusion.24 = (bf16[2,384,384]{2,1,0:T(8,128)(2,1)}, f32[2,384,384]{2,1,0:T(8,128)}) fusion(f32[2,384,384]{2,1,0:T(8,128)S(1)} %bitcast.62, bf16[384,6144,1]{1,0,2:T(8,128)(2,1)} %reshape.59, bf16[2,6144,384]{2,1,0:T(8,128)(2,1)} %all-gather.3.cloned.1.call-done), kind=kOutput, calls=%fused_computation.57 | convolution fusion | flops 3624468480 | bytes 17104896 | tf_op jit(solution)/shard_map/rk,skc->src/dot_general | solution.py:69
  465.8 0.8 copy-done.1
  466.6 0.3 convolution_bitcast_fusion
  467.0 203.9 %all-gather.5.cloned.1.call-done = bf16[2,6144,384]{2,1,0:T(8,128)(2,1)} async-done(((bf16[2,384,384]{2,1,0:T(8,128)(2,1)}), bf16[2,6144,384]{2,1,0:T(8,128)(2,1)}) %all-gather.5.cloned.1.call-update) | async-done | bytes 9437200 | tf_op jit(solution)/shard_map/all_gather | solution.py:68
  670.9 8.5 %fusion.1 = f32[2,384,384]{2,1,0:T(8,128)S(1)} fusion(f32[2,384,384]{2,1,0:T(8,128)S(1)} %bitcast.63, bf16[384,6144,1]{1,0,2:T(8,128)(2,1)} %reshape.59, bf16[2,6144,384]{2,1,0:T(8,128)(2,1)} %all-gather.5.cloned.1.call-done), kind=kOutput, calls=%fused_computation.6 | convolution fusion | flops 3624173568 | bytes 16515072 | tf_op jit(solution)/shard_map/rk,skc->src/dot_general | solution.py:69
  679.7 0.9 fusion.2
  (37 shorter events, 1.8 us)
Async XLA Ops:
  7.4 431.7 %all-reduce.3.cloned.1.call-start = ((), (), s32[]{:S(2)}) async-start(), calls=%async_computation.2 | async-start | bytes 393216 | tf_op jit(solution)/shard_map/psum | solution.py:40
  8.1 5.7 collective-permute-start.1
  12.4 4.6 collective-permute-start
  17.1 12.7 %collective-permute-start.2 = (f32[4,1,512]{2,1,0:T(1,128)S(1)}, f32[4,1,512]{2,1,0:T(1,128)S(1)}, u32[]{:S(2)}, u32[]{:S(2)}) collective-permute-start(f32[4,1,512]{2,1,0:T(1,128)S(1)} %get-tuple-element.10), channel_id=1, source_target_pairs={{1,0},{2,1},{3,2},{4,3},{5,4},{6,5},{7,6},{8,7},{9,8},{10,9},{11,1... | collective-permute-start | bytes 24584 | tf_op jit(solution)/shard_map/ppermute | solution.py:19
  20.9 8.9 %collective-permute-start.3 = (f32[4,1,512]{2,1,0:T(1,128)S(1)}, f32[4,1,512]{2,1,0:T(1,128)S(1)}, u32[]{:S(2)}, u32[]{:S(2)}) collective-permute-start(f32[4,1,512]{2,1,0:T(1,128)S(1)} %get-tuple-element.9), channel_id=1, source_target_pairs={{0,1},{1,2},{2,3},{3,4},{4,5},{5,6},{6,7},{7,8},{8,9},{9,10},{10,1... | collective-permute-start | bytes 24584 | tf_op jit(solution)/shard_map/ppermute | solution.py:16
  30.8 2.8 copy-start
  33.6 1.7 copy-start.2
  35.3 1.2 copy-start.5
  35.3 420.1 %all-gather.3.cloned.1.call-start = ((), (), s32[]{:S(2)}) async-start(), calls=%async_computation.1 | async-start | bytes 10027008 | tf_op jit(solution)/shard_map/all_gather | solution.py:68
  39.3 401.1 %all-to-all-start = ((bf16[16,384,384]{2,1,0:T(8,128)(2,1)}), bf16[16,384,384]{2,1,0:T(8,128)(2,1)}, u32[]{:S(2)}, u32[]{:S(2)}) async-start(bf16[16,384,384]{2,1,0:T(8,128)(2,1)} %stack.4), calls=%async_computation | async-start | bytes 9437184 | tf_op jit(solution)/shard_map/all_to_all | solution.py:72
  49.6 621.3 %all-gather.5.cloned.1.call-start = ((), (), s32[]{:S(2)}) async-start(), calls=%async_computation.3 | async-start | bytes 10027008 | tf_op jit(solution)/shard_map/all_gather | solution.py:68
  455.4 10.4 %copy-start.4 = (f32[3,128,128]{2,1,0:T(8,128)S(1)}, f32[3,128,128]{2,1,0:T(8,128)}, u32[]{:S(2)}) copy-start(f32[3,128,128]{2,1,0:T(8,128)} %all-reduce.3.cloned.1.call-done) | copy-start | bytes 589828
  465.5 1.1 copy-start.1
  670.9 8.5 %copy-start.3 = (f32[2,384,384]{2,1,0:T(8,128)S(1)}, f32[2,384,384]{2,1,0:T(8,128)}, u32[]{:S(2)}) copy-start(f32[2,384,384]{2,1,0:T(8,128)} %get-tuple-element.16) | copy-start | bytes 3538948
Sparse Core Ops, SparseCore 0:
  35.4 403.6 all-reduce.2
Sparse Core Ops, SparseCore 1:
  37.6 312.0 all-gather.2
  465.7 205.2 all-gather.4
